TPU v7x, 1024 devices: a whole 4x4x32 slice. The times are simulated.
1024 devices in a mesh: space: 512 (over x_hi, z, y, core), dp: 2 (over x_lo).
Axes of the slice: x: 4 (x_hi: 2, x_lo: 2; x = x_hi * 2 + x_lo), y: 4, z: 32, core: 2. Of those that a mesh axis runs over, the one named last changes fastest.
Arguments:
- node_features: float32 [2, 128, 131072], P('dp', None, 'space'), may hold values from -6 to 6
- positions: float32 [2, 3, 131072], P('dp', None, 'space')
- species: int32 [2, 131072], P('dp', 'space'), may hold values from 0 to 7
- energy_cotangent: float32 [2, 131072], P('dp', 'space'), may hold values from -6 to 6
- pair_target: int32 [2, 10240], P('dp', 'space'), may hold values from 0 to 3, as said below
- pair_source: int32 [2, 10240], P('dp', 'space'), may hold values from 0 to 7, as said below
- pair_count: int32 [2, 512], P('dp', 'space'), may hold values from 4 to 20, as said below
- radial_weight: float32 [8, 128], replicated, may hold values from -2 to 2
- mix_weight: bfloat16 [384, 128], replicated, may hold values from -0.3125 to 0.3125
- readout_weight: float32 [128], replicated, may hold values from -0.5 to 0.5
- species_shift: float32 [8], replicated, may hold values from -4 to 4
Outputs:
- atom_energy: float32 [2, 131072], P('dp', 'space')
- feature_grad: float32 [2, 128, 131072], P('dp', None, 'space')
- radial_grad: float32 [8, 128], replicated
- mix_grad: float32 [384, 128], replicated
- readout_grad: float32 [128], replicated
- shift_grad: float32 [8], replicated
Inputs may be any that keep to these rules, and one draw needn't show every extreme that they name: `pair_target`: the target cell of a slot lies in its slab. `pair_source`: A live slot's source cell lies within 2 cells of its target cell and inside the snapshot; every target cell pairs with itself; no pair appears twice in a slab. `pair_count`: counts differ from slab to slab; in every snapshot some slab uses all 20 slots.
All inputs are finite; a program needn't handle non-finite values.
Results may differ from a plain program's by a relative error of at most 0.0009.
The roundings to bfloat16 on the way count: a program that leaves them out, or rounds other values in their place, can miss the bound.
Values sent between devices are 32-bit elements; how exact they have to be, the bound alone decides.
A program may use at most 32 MiB of HBM per device.

v0:
```python
import math

import jax
import jax.numpy as jnp
from jax import lax
from jax.sharding import PartitionSpec as P

CH = 128
NB = 8
NSPEC = 8
CELL_ATOMS = 64
HALO_CELLS = 2


cutoff = 5.0
message_scale = 0.25


def padded(value, sides, width):
    for axis, dim in sides:
        peers, length = (lax.axis_size(axis), value.shape[dim])
        up = [(i, (i + 1) % peers) for i in range(peers - 1)]
        down = [(j, i) for i, j in up]
        last = lax.slice_in_dim(value, length - width, length, axis=dim)
        initial = lax.slice_in_dim(value, 0, width, axis=dim)
        before = lax.ppermute(last, axis, up)
        after = lax.ppermute(initial, axis, down)
        value = jnp.concatenate([before, value, after], axis=dim)
    return value


def from_behind(block, axis, distance):
    devices = range(lax.axis_size(axis))
    route = [(i - distance, i) for i in devices if i - distance in devices]
    return lax.ppermute(block, axis, route)


def harmonics(delta):
    delta_x = delta[0]
    delta_y = delta[1]
    delta_z = delta[2]
    square_dist = delta_x * delta_x + delta_y * delta_y + delta_z * delta_z
    root_three = math.sqrt(3.0)
    root_fifteen = math.sqrt(15.0)
    root_five = math.sqrt(5.0)
    return jnp.stack(
        [
            jnp.ones_like(delta_x),
            root_three * delta_x,
            root_three * delta_y,
            root_three * delta_z,
            root_fifteen * delta_x * delta_y,
            root_fifteen * delta_y * delta_z,
            0.5 * root_five * (3.0 * delta_z * delta_z - square_dist),
            root_fifteen * delta_x * delta_z,
            0.5 * root_fifteen * (delta_x * delta_x - delta_y * delta_y),
        ]
    )


def edge_table(target_coords, source_coords, self_block):
    delta = (target_coords[:, :, None] - source_coords[:, None, :]) / cutoff
    square_dist = jnp.sum(delta * delta, axis=0)
    distance = jnp.sqrt(square_dist)
    envelope = jnp.square(jnp.maximum(1.0 - square_dist, 0.0))
    envelope = envelope * (1.0 - self_block * jnp.eye(CELL_ATOMS, dtype=jnp.float32))
    orders = jnp.arange(1, NB + 1).astype(jnp.float32)
    radial = jnp.sinc(orders[:, None, None] * distance[None]) * envelope[None] * message_scale
    harmonic = harmonics(delta)
    radial_t = jnp.transpose(radial, (0, 2, 1))
    harmonic_t = jnp.transpose(harmonic, (2, 0, 1))
    factor = radial_t[:, :, None, :] * harmonic_t[None]
    return factor.reshape(NB * CELL_ATOMS, 9 * CELL_ATOMS).astype(jnp.bfloat16)


def keep_same(values):
    return values


def pair_pass(
    totals,
    source_rows,
    source_coords,
    target_coords,
    first_cell,
    targets,
    sources,
    live_pairs,
    select,
):

    def visit(index, current):
        tcell = targets[index]
        scell = sources[index]

        def visit_add(values):
            tco = lax.dynamic_slice_in_dim(target_coords, tcell * CELL_ATOMS, CELL_ATOMS, 1)
            sco = lax.dynamic_slice_in_dim(
                source_coords, (scell - first_cell) * CELL_ATOMS, CELL_ATOMS, 1
            )
            factor = edge_table(tco, sco, (scell == tcell + HALO_CELLS).astype(jnp.float32))
            block = lax.dynamic_slice_in_dim(
                source_rows, (scell - first_cell) * CELL_ATOMS, CELL_ATOMS, 2
            )
            product = jnp.dot(
                block.reshape(CH, NB * CELL_ATOMS), factor, preferred_element_type=jnp.float32
            )
            before = lax.dynamic_slice_in_dim(values, tcell * CELL_ATOMS, CELL_ATOMS, 2)
            return lax.dynamic_update_slice_in_dim(
                values, before + product.reshape(CH, 9, CELL_ATOMS), tcell * CELL_ATOMS, 2
            )

        return lax.cond((index < live_pairs) & select(scell), visit_add, keep_same, current)

    return lax.fori_loop(0, targets.shape[0], visit, totals)


def body(
    node_features,
    positions,
    species,
    energy_cotangent,
    pair_target,
    pair_source,
    pair_count,
    radial_weight,
    mix_weight,
    readout_weight,
    species_shift,
):
    features = node_features[0]
    coords = positions[0]
    species_here = species[0]
    energy_grad = energy_cotangent[0]
    targets = pair_target[0]
    sources = pair_source[0]
    live_pairs = pair_count[0, 0]
    atoms_here = features.shape[1]
    margin = HALO_CELLS * CELL_ATOMS
    weight_t = radial_weight.T
    scaled = (features[:, None, :] * weight_t[:, :, None]).astype(jnp.bfloat16)
    features_ext, coords_ext = (
        padded(features, (("space", 1),), margin),
        padded(coords, (("space", 1),), margin),
    )
    ghost_before = (features_ext[:, None, :margin] * weight_t[:, :, None]).astype(jnp.bfloat16)
    ghost_after = (features_ext[:, None, margin + atoms_here :] * weight_t[:, :, None]).astype(
        jnp.bfloat16
    )
    scaled_ext = jnp.concatenate([ghost_before, scaled, ghost_after], axis=2)
    messages = jnp.zeros((CH, 9, atoms_here), jnp.float32)

    def every_cell(scell):
        return scell >= 0

    messages = pair_pass(
        messages, scaled_ext, coords_ext, coords, 0, targets, sources, live_pairs, every_cell
    )
    invariants = jnp.concatenate(
        [
            messages[:, 0],
            0.5 * jnp.sum(messages[:, 1:4] ** 2, axis=1),
            0.5 * jnp.sum(messages[:, 4:9] ** 2, axis=1),
        ],
        axis=0,
    ).astype(jnp.bfloat16)
    preact = lax.dot_general(
        mix_weight, invariants, (((0,), (0,)), ((), ())), preferred_element_type=jnp.float32
    )
    gating = jax.nn.sigmoid(preact)
    updated = features + preact * gating
    onehot = (species_here[None, :] == jnp.arange(NSPEC)[:, None]).astype(jnp.float32)
    energy = jnp.sum(updated * readout_weight[:, None], axis=0) + jnp.sum(
        onehot * species_shift[:, None], axis=0
    )
    grad_out = jnp.sum(updated * energy_grad[None, :], axis=1)
    grad_shift = jnp.sum(onehot * energy_grad[None, :], axis=1)
    grad_pre = (
        energy_grad[None, :] * readout_weight[:, None] * gating * (1.0 + preact * (1.0 - gating))
    ).astype(jnp.bfloat16)
    grad_mix = lax.dot_general(
        invariants, grad_pre, (((1,), (1,)), ((), ())), preferred_element_type=jnp.float32
    )
    grad_inv = jnp.dot(mix_weight, grad_pre, preferred_element_type=jnp.float32)
    grad_msg = jnp.concatenate(
        [
            grad_inv[:CH][:, None],
            grad_inv[CH : 2 * CH][:, None] * messages[:, 1:4],
            grad_inv[2 * CH :][:, None] * messages[:, 4:9],
        ],
        axis=1,
    ).astype(jnp.bfloat16)

    def revisit(index, current):
        tcell = targets[index]
        scell = sources[index]

        def revisit_add(values):
            tco = lax.dynamic_slice_in_dim(coords, tcell * CELL_ATOMS, CELL_ATOMS, 1)
            sco = lax.dynamic_slice_in_dim(coords_ext, scell * CELL_ATOMS, CELL_ATOMS, 1)
            factor = edge_table(tco, sco, (scell == tcell + HALO_CELLS).astype(jnp.float32))
            block = lax.dynamic_slice_in_dim(grad_msg, tcell * CELL_ATOMS, CELL_ATOMS, 2).reshape(
                CH, 9 * CELL_ATOMS
            )
            product = lax.dot_general(
                block, factor, (((1,), (1,)), ((), ())), preferred_element_type=jnp.float32
            )
            before = lax.dynamic_slice_in_dim(values, scell * CELL_ATOMS, CELL_ATOMS, 2)
            return lax.dynamic_update_slice_in_dim(
                values, before + product.reshape(CH, NB, CELL_ATOMS), scell * CELL_ATOMS, 2
            )

        return lax.cond(index < live_pairs, revisit_add, keep_same, current)

    grad_scaled = lax.fori_loop(
        0, targets.shape[0], revisit, jnp.zeros((CH, NB, atoms_here + 2 * margin), jnp.float32)
    )
    grad_ext = jnp.sum(grad_scaled * weight_t[:, :, None], axis=1)
    grad_radial = jnp.sum(grad_scaled * features_ext[:, None, :], axis=2).T
    from_after = from_behind(grad_ext[:, :margin], "space", -1)
    from_before = from_behind(grad_ext[:, margin + atoms_here :], "space", 1)
    feature_grad = (
        readout_weight[:, None] * energy_grad[None, :] + grad_ext[:, margin : margin + atoms_here]
    )
    feature_grad = feature_grad + jnp.pad(from_before, ((0, 0), (0, atoms_here - margin)))
    feature_grad = feature_grad + jnp.pad(from_after, ((0, 0), (atoms_here - margin, 0)))
    grad_radial, grad_mix, grad_out, grad_shift = lax.psum(
        (grad_radial, grad_mix, grad_out, grad_shift), ("space", "dp")
    )
    scale = 1.0 / math.sqrt(atoms_here * lax.axis_size("space") * lax.axis_size("dp"))
    return (
        energy[None],
        feature_grad[None],
        grad_radial * scale,
        grad_mix * scale,
        grad_out * scale,
        grad_shift * scale,
    )


def solution(mesh):
    return jax.shard_map(
        body,
        mesh=mesh,
        in_specs=(
            P("dp", None, "space"),
            P("dp", None, "space"),
            P("dp", "space"),
            P("dp", "space"),
            P("dp", "space"),
            P("dp", "space"),
            P("dp", "space"),
            P(),
            P(),
            P(),
            P(),
        ),
        out_specs=(P("dp", "space"), P("dp", None, "space"), P(), P(), P(), P()),
        check_vma=False,
    )
```

profile of v0, /device:TPU:1, one launch (start us, length us, event | category | flops | bytes accessed | tf_op | source)
XLA Modules:
  0.0 1187.6 jit_solution(1423750432420451807)
XLA Ops:
  7.2 1.0 copy.28
  8.2 4.6 collective-permute-start
  12.8 12.8 %collective-permute-start.1 = (f32[128,128]{0,1:T(8,128)S(1)}, f32[128,128]{0,1:T(8,128)S(1)}, u32[]{:S(2)}, u32[]{:S(2)}) collective-permute-start(f32[128,128]{0,1:T(8,128)S(1)} %get-tuple-element.478), channel_id=1, source_target_pairs={{2,0},{4,2},{6,4},{8,6},{10,8},{12,10},{14,12},{16,14},{18,16},{20... | collective-permute-start | bytes 196616 | tf_op jit(solution)/shard_map/ppermute | solution.py:27
  25.6 0.7 copy.35
  26.3 1.9 collective-permute-start.2
  28.2 2.4 collective-permute-start.3
  30.6 0.8 multiply_convert_fusion.9
  31.4 0.9 select_reduce_fusion
  32.3 0.8 collective-permute-done.3
  33.2 0.8 multiply_convert_fusion.12
  34.0 1.0 pad_maximum_fusion
  35.1 94.0 %while.32 = (s32[]{:T(128)}, f32[128,9,256]{0,2,1:T(8,128)S(1)}, s32[]{:T(128)}, s32[20]{0:T(128)S(1)}, s32[20]{0:T(128)S(1)}, /*index=5*/bf16[128,8,512]{0,2,1:...) while((s32[]{:T(128)}, f32[128,9,256]{0,2,1:T(8,128)S(1)}, s32[]{:T(128)}, ...), condition=%wide.region_4.6_spmd, body=%wide.region_0.5_spmd.sunk | while | flops 77504544 | bytes 4658081 | solution.py:115
  37.0 6.2 conditional.4
  41.2 0.7 convert_element_type.70
  41.9 0.9 constant_dynamic-slice_fusion.2
  45.1 6.2 conditional.4
  49.3 0.7 convert_element_type.70
  50.0 0.9 constant_dynamic-slice_fusion.2
  53.2 6.2 conditional.4
  57.4 0.7 convert_element_type.70
  58.1 0.9 constant_dynamic-slice_fusion.2
  61.3 6.2 conditional.4
  65.5 0.7 convert_element_type.70
  66.2 0.9 constant_dynamic-slice_fusion.2
  69.4 6.2 conditional.4
  73.6 0.7 convert_element_type.70
  74.3 0.9 constant_dynamic-slice_fusion.2
  77.4 6.2 conditional.4
  78.1 0.6 dynamic_slice.61
  81.6 0.7 convert_element_type.70
  82.4 0.9 constant_dynamic-slice_fusion.2
  85.5 6.2 conditional.4
  86.2 0.6 dynamic_slice.61
  89.7 0.7 convert_element_type.70
  90.4 0.9 constant_dynamic-slice_fusion.2
  93.6 6.2 conditional.4
  94.3 0.6 dynamic_slice.61
  97.8 0.7 convert_element_type.70
  98.5 0.9 constant_dynamic-slice_fusion.2
  101.7 6.2 conditional.4
  105.9 0.7 convert_element_type.70
  106.6 0.9 constant_dynamic-slice_fusion.2
  130.4 58.4 %while.33 = (s32[]{:T(128)}, f32[128,8,512]{0,2,1:T(8,128)S(1)}, s32[]{:T(128)}, s32[20]{0:T(128)S(1)}, s32[20]{0:T(128)S(1)}, /*index=5*/bf16[128,9,256]{0,2,1:...) while((s32[]{:T(128)}, f32[128,8,512]{0,2,1:T(8,128)S(1)}, s32[]{:T(128)}, ...), condition=%wide.region_13.15_spmd, body=%wide.region_9.14_spmd.sunk | while | flops 77496344 | bytes 2265997 | solution.py:215
  131.1 5.0 conditional.5
  136.7 5.0 conditional.5
  136.7 0.6 dynamic_slice.69
  142.4 5.0 conditional.5
  143.6 0.6 dynamic_slice.67
  148.0 5.0 conditional.5
  153.7 5.0 conditional.5
  154.9 0.6 dynamic_slice.67
  159.3 5.0 conditional.5
  165.0 5.0 conditional.5
  170.6 5.0 conditional.5
  176.3 5.0 conditional.5
  189.2 102.5 %collective-permute-start.4 = (f32[128,128]{0,1:T(8,128)S(1)}, f32[128,128]{0,1:T(8,128)S(1)}, u32[]{:S(2)}, u32[]{:S(2)}) collective-permute-start(f32[128,128]{0,1:T(8,128)S(1)} %get-tuple-element.475), channel_id=1, source_target_pairs={{0,2},{2,4},{4,6},{6,8},{8,10},{10,12},{12,14},{14,16},{16,18},{18... | collective-permute-start | bytes 196616 | tf_op jit(solution)/shard_map/ppermute | solution.py:35
  291.8 1.9 collective-permute-start.5
  293.7 1.0 fusion.73
  294.7 2.6 collective-permute-done.5
  297.5 189.9 %all-reduce.2 = (f32[8,128]{1,0:T(8,128)S(1)}, f32[128]{0:T(128)S(1)}, f32[8]{0:T(128)S(1)}) all-reduce(f32[8,128]{1,0:T(8,128)S(1)} %bitcast.75, f32[128]{0:T(128)S(1)} %get-tuple-element.422, f32[8]{0:T(128)S(1)} %get-tuple-element.424), channel_id=1, replica_groups=mesh['space'=512,'dp'=2] {'space','dp'}, use_global_device_ids=true, to_apply=%region_16.18 | all-reduce | flops 1160 | bytes 9280 | tf_op jit(solution)/shard_map/psum | solution.py:227
  487.4 0.6 broadcast_multiply_fusion.1
  489.0 0.8 copy.29
  490.3 688.8 %all-reduce.5.cloned.1.call-done = f32[384,128]{1,0:T(8,128)} async-done(((f32[384,128]{1,0:T(8,128)}), f32[384,128]{1,0:T(8,128)}) %all-reduce.5.cloned.1.call-update) | async-done | bytes 196624 | tf_op jit(solution)/shard_map/psum | solution.py:227
  1179.1 1.6 broadcast_multiply_fusion
  (383 shorter events, 48.6 us)
Async XLA Ops:
  7.2 122.1 %copy-start = (bf16[384,128]{1,0:T(8,128)(2,1)S(1)}, bf16[384,128]{1,0:T(8,128)(2,1)}, u32[]{:S(2)}) copy-start(bf16[384,128]{1,0:T(8,128)(2,1)} %param.28) | copy-start | bytes 294916
  7.2 1172.0 %all-reduce.5.cloned.1.call-start = ((), (), s32[]{:S(2)}) async-start(), calls=%async_computation | async-start | bytes 393216 | tf_op jit(solution)/shard_map/psum | solution.py:227
  8.2 24.9 %collective-permute-start = (f32[128,128]{0,1:T(8,128)S(1)}, f32[128,128]{0,1:T(8,128)S(1)}, u32[]{:S(2)}, u32[]{:S(2)}) collective-permute-start(f32[128,128]{0,1:T(8,128)S(1)} %get-tuple-element.477), channel_id=1, source_target_pairs={{0,2},{2,4},{4,6},{6,8},{8,10},{10,12},{12,14},{14,16},{16,18},{18... | collective-permute-start | bytes 196616 | tf_op jit(solution)/shard_map/ppermute | solution.py:26
  12.8 20.3 %collective-permute-start.1 = (f32[128,128]{0,1:T(8,128)S(1)}, f32[128,128]{0,1:T(8,128)S(1)}, u32[]{:S(2)}, u32[]{:S(2)}) collective-permute-start(f32[128,128]{0,1:T(8,128)S(1)} %get-tuple-element.478), channel_id=1, source_target_pairs={{2,0},{4,2},{6,4},{8,6},{10,8},{12,10},{14,12},{16,14},{18,16},{20... | collective-permute-start | bytes 196616 | tf_op jit(solution)/shard_map/ppermute | solution.py:27
  26.3 6.0 collective-permute-start.2
  28.2 4.9 collective-permute-start.3
  31.4 3.7 copy-start.4
  31.4 3.7 copy-start.5
  129.1 0.7 copy-start.2
  129.1 0.7 copy-start.3
  130.4 58.5 %copy-start.1 = (f32[8,128]{1,0:T(8,128)S(1)}, f32[8,128]{1,0:T(8,128)}, u32[]{:S(2)}) copy-start(f32[8,128]{1,0:T(8,128)} %param.27) | copy-start | bytes 12292
  189.2 105.5 %collective-permute-start.4 = (f32[128,128]{0,1:T(8,128)S(1)}, f32[128,128]{0,1:T(8,128)S(1)}, u32[]{:S(2)}, u32[]{:S(2)}) collective-permute-start(f32[128,128]{0,1:T(8,128)S(1)} %get-tuple-element.475), channel_id=1, source_target_pairs={{0,2},{2,4},{4,6},{6,8},{8,10},{10,12},{12,14},{14,16},{16,18},{18... | collective-permute-start | bytes 196616 | tf_op jit(solution)/shard_map/ppermute | solution.py:35
  291.8 5.6 collective-permute-start.5
Sparse Core Ops, SparseCore 0:
  294.8 884.2 all-reduce.4
where the time goes:
time: 1190 us
  waiting for transfers between devices  692 us (58%)
  blocking collectives  190 us (16%)
  starting transfers between devices  126 us (11%)
  loops' own time  89.5 us (8%)
  local copies, waits for them, and re-layouts  46.8 us (4%)
  other arithmetic  20.6 us (2%)
  between operations  14.3 us (1%)
    psum x1, waiting for transfers between devices, body(): lax.psum((grad_radial, grad_mix, grad_out, grad_shift), ('space', 'dp'))  689 us
    psum x1, blocking collectives, body(): lax.psum((grad_radial, grad_mix, grad_out, grad_shift), ('space', 'dp'))  190 us
    ppermute x2, starting transfers between devices, from_behind(): return lax.ppermute(block, axis, route)  104 us
    another operation x1, loops' own time, pair_pass(): return lax.fori_loop(0, targets.shape[0], visit, totals)  26.5 us
    another operation x20, loops' own time, visit(): lax.cond((index < live_pairs) & select(scell), visit_add, keep_same, curr...  24.8 us
    another operation x20, loops' own time, revisit(): return lax.cond(index < live_pairs, revisit_add, keep_same, current)  24.7 us
  transfers between devices with their start and end apart: 7, of which 3 were waited for; matrix products, arithmetic and copies ran while one was open for 1% of the time, Pallas kernels for 0%

commit v1 on v0

v1 whole, which is shorter than its diff:
```python
import functools
import math

import jax
import jax.numpy as jnp
from jax import lax
from jax.experimental import pallas as pl
from jax.experimental.pallas import tpu as pltpu
from jax.sharding import PartitionSpec as P

CH = 128
NB = 8
NY = 9
NSPEC = 8
CELL = 64
BLK = 128
F32 = jnp.float32
BF16 = jnp.bfloat16
MESH = pl.DeviceIdType.MESH

SPLIT = {"xh": 2, "z": 32, "zlo": 4, "y": 4, "core": 2}
ROWS = 512

COS_TERMS = [(-1.0) ** k * math.pi ** (2 * k) / math.factorial(2 * k) for k in range(11)]
SINC_TERMS = [(-1.0) ** k * math.pi ** (2 * k) / math.factorial(2 * k + 1) for k in range(10)]


def horner(terms, x):
    total = x * terms[-1] + terms[-2]
    for term in reversed(terms[:-2]):
        total = total * x + term
    return total


def nt_dot(a, b):
    return lax.dot_general(a, b, (((1,), (1,)), ((), ())), preferred_element_type=F32)


def nn_dot(a, b):
    return jnp.dot(a, b, preferred_element_type=F32)


def column(row):
    return jnp.transpose(jnp.broadcast_to(row, (BLK, BLK)))


def kernel(
    dims,
    feat_ref,
    pos_ref,
    spec_ref,
    eg_ref,
    pt_ref,
    ps_ref,
    pc_ref,
    w_ref,
    mix_ref,
    ro_ref,
    sh_ref,
    energy_ref,
    fgrad_ref,
    rad_ref,
    mixg_ref,
    rog_ref,
    shg_ref,
    table,
    scaled,
    feats,
    scol,
    wcol,
    live,
    msg,
    gmsg,
    inv,
    racc,
    gext,
    halo_out,
    halo_in,
    grad_in,
    big_src,
    big_rs,
    z_a,
    z_b,
    z_as,
    z_bs,
    big_ag,
    sm_src,
    sm_pl,
    sm_sum,
    sm_x,
    sm_z,
    send_sem,
    recv_sem,
):
    nsp, ndp, nxh, nz, zlo, ny, nco = dims
    plane = nxh * ndp * ny * nco
    zhi = nz // zlo
    sp = lax.axis_index("space")
    dp = lax.axis_index("dp")
    core = sp % nco
    yy = (sp // nco) % ny
    zz = (sp // (nco * ny)) % nz
    xh = sp // (nco * ny * nz)
    me = ((xh * ndp + dp) * ny + yy) * nco + core

    def at_plane(g):
        return (
            ((g // (nco * ny * ndp)) * nz + zz) * (ny * nco) + g % (nco * ny),
            (g // (nco * ny)) % ndp,
        )

    def at_z(z):
        return ((xh * nz + z) * ny + yy) * nco + core, dp

    def plane_peer(k):
        return (me + k) % plane

    def za_peer(k):
        return (zz // zlo) * zlo + (zz % zlo + k) % zlo

    def zb_peer(k):
        return ((zz // zlo + k) % zhi) * zlo + zz % zlo

    def remote(src, dst, n, dev):
        return pltpu.make_async_remote_copy(
            src_ref=src,
            dst_ref=dst,
            send_sem=send_sem.at[n],
            recv_sem=recv_sem.at[n],
            device_id=dev,
            device_id_type=MESH,
        )

    barrier = pltpu.get_barrier_semaphore()

    def greet(dev):
        pl.semaphore_signal(barrier, inc=1, device_id=dev, device_id_type=MESH)

    has_left = sp > 0
    has_right = sp < nsp - 1

    @pl.when(has_left)
    def _():
        greet((sp - 1, dp))

    @pl.when(has_right)
    def _():
        greet((sp + 1, dp))

    def greet_plane(k, c):
        greet(at_plane(plane_peer(k)))
        return c

    lax.fori_loop(1, plane, greet_plane, 0)
    for k in range(1, zlo):
        greet(at_z(za_peer(k)))
    for k in range(1, zhi):
        greet(at_z(zb_peer(k)))

    @pl.when(me > 0)
    def _():
        greet(at_z((zz + me) % nz))
        greet(at_z((zz + nz - me) % nz))

    features = feat_ref[0]
    for s in range(2):
        halo_out[s, 0:CH, :] = features[:, s * BLK : (s + 1) * BLK]
        halo_out[s, CH : CH + 3, :] = pos_ref[0, :, s * BLK : (s + 1) * BLK]
        halo_out[s, CH + 3 : CH + 8, :] = jnp.zeros((5, BLK), F32)
        feats[1 + s] = features[:, s * BLK : (s + 1) * BLK]
        for d in range(3):
            scol[1 + s, d] = column(pos_ref[0, d : d + 1, s * BLK : (s + 1) * BLK])

    for b in range(NB):
        wcol[b] = column(w_ref[b : b + 1, :])
    for s in range(2):
        for b in range(NB):
            scaled[1 + s, :, b * BLK : (b + 1) * BLK] = (feats[1 + s] * wcol[b]).astype(BF16)

    slots = pt_ref.shape[1]
    used = lax.broadcasted_iota(jnp.int32, (1, slots), 1) < pc_ref[...]
    hit_source = ps_ref[...] == lax.broadcasted_iota(jnp.int32, (8, slots), 0)
    lane = lax.broadcasted_iota(jnp.int32, (8, BLK), 1)
    for t in range(2):
        cols = []
        for h in range(2):
            hit = hit_source & (used & (pt_ref[...] == 2 * t + h))
            cols.append(jnp.sum(jnp.where(hit, 1.0, 0.0), axis=1, keepdims=True))
        live[t] = jnp.where(lane < CELL, cols[0], cols[1])

    msg[...] = jnp.zeros_like(msg)

    root3 = math.sqrt(3.0)
    root15 = math.sqrt(15.0)
    root5 = math.sqrt(5.0)
    sub16 = lax.broadcasted_iota(jnp.int32, (16, BLK), 0)
    lane16 = lax.broadcasted_iota(jnp.int32, (16, BLK), 1)

    def produce(p, t, s):
        lanes = pl.ds(pl.multiple_of(t * BLK, BLK), BLK)
        targets = [jnp.broadcast_to(pos_ref[0, d : d + 1, lanes], (16, BLK)) for d in range(3)]
        shift = jnp.where(s == t + 1, 0, 2 * BLK)

        def chunk(q, c):
            r0 = pl.multiple_of(q * 16, 16)
            rows = pl.ds(r0, 16)
            ux, uy, uz = [(targets[d] - scol[s, d, rows, :]) * 0.2 for d in range(3)]
            square = ux * ux + uy * uy + uz * uz
            alive = jnp.broadcast_to(live[t, pl.ds(2 * s + q // 4, 1), :], (16, BLK)) > 0.5
            keep = (square < 1.0) & alive & (sub16 + (r0 + shift) != lane16)
            square = jnp.where(keep, square, 1.0)
            ux = jnp.where(keep, ux, 0.0)
            uy = jnp.where(keep, uy, 0.0)
            uz = jnp.where(keep, uz, 0.0)
            cosine2 = 2.0 * horner(COS_TERMS, square)
            gap = 1.0 - square
            base = (gap * gap) * (0.25 * horner(SINC_TERMS, square))
            ux15 = root15 * ux
            harmonic = [
                None,
                root3 * ux,
                root3 * uy,
                root3 * uz,
                ux15 * uy,
                root15 * uy * uz,
                (0.5 * root5) * (3.0 * uz * uz - square),
                ux15 * uz,
                (0.5 * root15) * (ux * ux - uy * uy),
            ]
            older, newer = None, base
            for b in range(NB):
                radial = newer * (1.0 / (b + 1)) if b else newer
                at = pl.ds(b * BLK + r0, 16)
                for y in range(NY):
                    value = radial * harmonic[y] if y else radial
                    table[p, at, y * BLK : (y + 1) * BLK] = value.astype(BF16)
                following = cosine2 * newer - older if b else cosine2 * newer
                older, newer = newer, following
            return c

        lax.fori_loop(0, BLK // 16, chunk, 0)

    def forward(p, t, s):
        produce(p, t, s)
        msg[t] += nn_dot(scaled[s], table[p])

    forward(1, 0, 1)

    total = plane - 1 + (zlo - 1) + (zhi - 1)
    total = total + has_left.astype(jnp.int32) + has_right.astype(jnp.int32)
    total = total + 2 * (me > 0).astype(jnp.int32)
    pl.semaphore_wait(barrier, total)

    to_left = remote(halo_out.at[0], halo_in.at[1], 0, (sp - 1, dp))
    to_right = remote(halo_out.at[1], halo_in.at[0], 1, (sp + 1, dp))

    @pl.when(has_left)
    def _():
        to_left.start()

    @pl.when(has_right)
    def _():
        to_right.start()

    def inner(p, c):
        forward(p, (p - 1) // 2, 1 + (p - 1) % 2)
        return c

    lax.fori_loop(2, 5, inner, 0)

    @pl.when(has_left)
    def _():
        to_right.wait_recv()

    @pl.when(has_right)
    def _():
        to_left.wait_recv()

    @pl.when(jnp.logical_not(has_left))
    def _():
        halo_in[0] = jnp.zeros((CH + 8, BLK), F32)

    @pl.when(jnp.logical_not(has_right))
    def _():
        halo_in[1] = jnp.zeros((CH + 8, BLK), F32)

    for h, s in ((0, 0), (1, 3)):
        feats[s] = halo_in[h, 0:CH, :]
        for d in range(3):
            scol[s, d] = column(halo_in[h, CH + d : CH + d + 1, :])
        for b in range(NB):
            scaled[s, :, b * BLK : (b + 1) * BLK] = (feats[s] * wcol[b]).astype(BF16)

    def outer(h, c):
        forward(5 * h, h, 3 * h)
        return c

    lax.fori_loop(0, 2, outer, 0)

    mix = mix_ref[...]
    mix_t = jnp.concatenate(
        [jnp.transpose(mix[k * CH : (k + 1) * CH].astype(F32)) for k in range(3)], axis=1
    ).astype(BF16)
    ro_col = column(ro_ref[...])
    lane_ch = lax.broadcasted_iota(jnp.int32, (CH, BLK), 1)
    row_sp = lax.broadcasted_iota(jnp.int32, (NSPEC, BLK), 0)
    shift_col = jnp.transpose(jnp.broadcast_to(sh_ref[...], (NSPEC, NSPEC)))[:, 0:1]
    for t in range(2):
        lanes = slice(t * BLK, (t + 1) * BLK)
        inv[0:CH, lanes] = msg[t, :, 0:BLK].astype(BF16)
        for k, ys in ((1, range(1, 4)), (2, range(4, 9))):
            acc = None
            for y in ys:
                m = msg[t, :, y * BLK : (y + 1) * BLK]
                acc = m * m if acc is None else acc + m * m
            inv[k * CH : (k + 1) * CH, lanes] = (0.5 * acc).astype(BF16)
    mixg = jnp.zeros((3 * CH, CH), F32)
    rog = jnp.zeros((CH, BLK), F32)
    shg = jnp.zeros((NSPEC, BLK), F32)
    for t in range(2):
        lanes = slice(t * BLK, (t + 1) * BLK)
        invariants = inv[:, lanes]
        preact = nn_dot(mix_t, invariants)
        gate = 1.0 / (1.0 + jnp.exp(-preact))
        updated = feats[1 + t] + preact * gate
        eg = eg_ref[:, lanes]
        onehot = (spec_ref[:, lanes] == row_sp).astype(F32)
        energy_ref[:, lanes] = jnp.sum(updated * ro_col, axis=0, keepdims=True) + jnp.sum(
            onehot * shift_col, axis=0, keepdims=True
        )
        rog += updated * eg
        shg += onehot * eg
        base = eg * ro_col
        gext[1 + t] = base
        gpre = (base * gate * (1.0 + preact * (1.0 - gate))).astype(BF16)
        mixg += nt_dot(invariants, gpre)
        ginv = nn_dot(mix, gpre)
        gmsg[t, :, 0:BLK] = ginv[0:CH].astype(BF16)
        for y in range(1, NY):
            k = 1 if y < 4 else 2
            gmsg[t, :, y * BLK : (y + 1) * BLK] = (
                ginv[k * CH : (k + 1) * CH] * msg[t, :, y * BLK : (y + 1) * BLK]
            ).astype(BF16)

    per = ROWS // plane
    tail = jnp.concatenate(
        [
            jnp.sum(jnp.transpose(rog), axis=0, keepdims=True),
            jnp.zeros((7, BLK), F32),
            jnp.sum(jnp.transpose(jnp.concatenate([shg, jnp.zeros((CH - NSPEC, BLK), F32)], axis=0)), axis=0, keepdims=True),
            jnp.zeros((ROWS - 3 * CH - 9, BLK), F32),
        ],
        axis=0,
    )
    big_src[...] = jnp.concatenate([mixg, tail], axis=0).reshape(plane, per, CH)

    def send_plane(src, dst, n):
        def step(k, c):
            g = plane_peer(k)
            remote(src(g), dst, n, at_plane(g)).start()
            return c

        lax.fori_loop(1, plane, step, 0)

    def wait_slots(buf, n, count, dev):
        part = buf.at[pl.ds(0, count)]
        copies = remote(part, part, n, dev)
        return copies

    big_rs[me] = big_src[me]
    send_plane(lambda g: big_src.at[g], big_rs.at[me], 2)

    racc[...] = jnp.zeros_like(racc)

    def backward(s, parts):
        def step(n, c):
            rows = pl.ds(pl.multiple_of(n * 256, 256), 256)
            g = nt_dot(gmsg[parts[0][1]], table[parts[0][0], rows, :])
            for p, t in parts[1:]:
                g += nt_dot(gmsg[t], table[p, rows, :])
            here = feats[s]
            add = gext[s]
            for h in range(2):
                gb = g[:, h * BLK : (h + 1) * BLK]
                add += gb * wcol[2 * n + h]
                racc[2 * n + h] += gb * here
            gext[s] = add
            return c

        lax.fori_loop(0, NB // 2, step, 0)

    gext[0] = jnp.zeros((CH, BLK), F32)
    gext[3] = jnp.zeros((CH, BLK), F32)
    backward(0, [(0, 0)])
    backward(3, [(5, 1)])

    back_left = remote(gext.at[0], grad_in.at[1], 3, (sp - 1, dp))
    back_right = remote(gext.at[3], grad_in.at[0], 4, (sp + 1, dp))

    @pl.when(has_left)
    def _():
        back_left.start()

    @pl.when(has_right)
    def _():
        back_right.start()

    any_plane = at_plane(plane_peer(1))
    any_a = at_z(za_peer(1))
    any_b = at_z(zb_peer(1))

    wait_slots(big_rs, 2, plane - 1, any_plane).wait_recv()
    z_as[...] = jnp.sum(big_rs[...], axis=0)
    z_a[zz % zlo] = z_as[...]
    for k in range(1, zlo):
        remote(z_as, z_a.at[zz % zlo], 5, at_z(za_peer(k))).start()

    backward(1, [(1, 0), (3, 1)])

    wait_slots(z_a, 5, zlo - 1, any_a).wait_recv()
    z_bs[...] = jnp.sum(z_a[...], axis=0)
    z_b[zz // zlo] = z_bs[...]
    for k in range(1, zhi):
        remote(z_bs, z_b.at[zz // zlo], 6, at_z(zb_peer(k))).start()

    backward(2, [(2, 0), (4, 1)])

    sm_src[...] = jnp.concatenate(
        [jnp.sum(jnp.transpose(racc[b]), axis=0, keepdims=True) for b in range(NB)], axis=0
    )
    sm_pl[me] = sm_src[...]
    send_plane(lambda g: sm_src, sm_pl.at[me], 7)

    wait_slots(z_b, 6, zhi - 1, any_b).wait_recv()
    big_ag[me] = jnp.sum(z_b[...], axis=0)
    send_plane(lambda g: big_ag.at[me], big_ag.at[me], 8)

    wait_slots(sm_pl, 7, plane - 1, any_plane).wait_recv()
    sm_sum[...] = jnp.sum(sm_pl[...], axis=0)
    slot = (zz + me) % nz
    to_z = remote(sm_sum, sm_x, 9, at_z((zz + nz - me) % nz))

    @pl.when(me > 0)
    def _():
        to_z.start()
        to_z.wait_recv()

    @pl.when(me == 0)
    def _():
        sm_x[...] = sm_sum[...]

    sm_z[slot] = sm_x[...]
    send_plane(lambda g: sm_x, sm_z.at[slot], 10)

    @pl.when(has_left)
    def _():
        back_right.wait_recv()
        gext[1] += grad_in[0]

    @pl.when(has_right)
    def _():
        back_left.wait_recv()
        gext[2] += grad_in[1]

    for t in range(2):
        fgrad_ref[0, :, t * BLK : (t + 1) * BLK] = gext[1 + t]

    scale = 1.0 / math.sqrt(2 * BLK * nsp * ndp)
    wait_slots(big_ag, 8, plane - 1, any_plane).wait_recv()
    whole = big_ag[...].reshape(ROWS, CH) * scale
    mixg_ref[...] = whole[0 : 3 * CH]
    rog_ref[...] = whole[3 * CH : 3 * CH + 1]
    shg_ref[...] = whole[3 * CH + 8 : 3 * CH + 9, 0:NSPEC]

    wait_slots(sm_z, 10, plane - 1, any_plane).wait_recv()
    rad_ref[...] = jnp.sum(sm_z[...], axis=0) * scale

    @pl.when(has_left)
    def _():
        to_left.wait_send()
        back_left.wait_send()

    @pl.when(has_right)
    def _():
        to_right.wait_send()
        back_right.wait_send()

    @pl.when(me > 0)
    def _():
        to_z.wait_send()

    wait_slots(big_rs, 2, plane - 1, any_plane).wait_send()
    wait_slots(z_a, 5, zlo - 1, any_a).wait_send()
    wait_slots(z_b, 6, zhi - 1, any_b).wait_send()
    wait_slots(sm_pl, 7, plane - 1, any_plane).wait_send()
    wait_slots(big_ag, 8, plane - 1, any_plane).wait_send()
    wait_slots(sm_z, 10, plane - 1, any_plane).wait_send()


def body(
    dims,
    node_features,
    positions,
    species,
    energy_cotangent,
    pair_target,
    pair_source,
    pair_count,
    radial_weight,
    mix_weight,
    readout_weight,
    species_shift,
):
    nsp, ndp, nxh, nz, zlo, ny, nco = dims
    plane = nxh * ndp * ny * nco
    zhi = nz // zlo
    per = ROWS // plane
    atoms = 2 * BLK
    vmem = pl.BlockSpec(memory_space=pltpu.VMEM)
    outs = pl.pallas_call(
        functools.partial(kernel, dims),
        out_shape=(
            jax.ShapeDtypeStruct((1, atoms), F32),
            jax.ShapeDtypeStruct((1, CH, atoms), F32),
            jax.ShapeDtypeStruct((NB, CH), F32),
            jax.ShapeDtypeStruct((3 * CH, CH), F32),
            jax.ShapeDtypeStruct((1, CH), F32),
            jax.ShapeDtypeStruct((1, NSPEC), F32),
        ),
        in_specs=[vmem] * 11,
        out_specs=(vmem,) * 6,
        scratch_shapes=[
            pltpu.VMEM((6, NB * BLK, NY * BLK), BF16),
            pltpu.VMEM((4, CH, NB * BLK), BF16),
            pltpu.VMEM((4, CH, BLK), F32),
            pltpu.VMEM((4, 3, BLK, BLK), F32),
            pltpu.VMEM((NB, CH, BLK), F32),
            pltpu.VMEM((2, 8, BLK), F32),
            pltpu.VMEM((2, CH, NY * BLK), F32),
            pltpu.VMEM((2, CH, NY * BLK), BF16),
            pltpu.VMEM((3 * CH, atoms), BF16),
            pltpu.VMEM((NB, CH, BLK), F32),
            pltpu.VMEM((4, CH, BLK), F32),
            pltpu.VMEM((2, CH + 8, BLK), F32),
            pltpu.VMEM((2, CH + 8, BLK), F32),
            pltpu.VMEM((2, CH, BLK), F32),
            pltpu.VMEM((plane, per, CH), F32),
            pltpu.VMEM((plane, per, CH), F32),
            pltpu.VMEM((zlo, per, CH), F32),
            pltpu.VMEM((zhi, per, CH), F32),
            pltpu.VMEM((per, CH), F32),
            pltpu.VMEM((per, CH), F32),
            pltpu.VMEM((plane, per, CH), F32),
            pltpu.VMEM((NB, CH), F32),
            pltpu.VMEM((plane, NB, CH), F32),
            pltpu.VMEM((NB, CH), F32),
            pltpu.VMEM((NB, CH), F32),
            pltpu.VMEM((nz, NB, CH), F32),
            pltpu.SemaphoreType.DMA((11,)),
            pltpu.SemaphoreType.DMA((11,)),
        ],
        compiler_params=pltpu.CompilerParams(
            collective_id=0, has_side_effects=True, vmem_limit_bytes=48 << 20
        ),
    )(
        node_features,
        positions,
        species,
        energy_cotangent,
        pair_target,
        pair_source,
        pair_count,
        radial_weight,
        mix_weight,
        readout_weight.reshape(1, CH),
        species_shift.reshape(1, NSPEC),
    )
    energy, feature_grad, grad_radial, grad_mix, grad_out, grad_shift = outs
    return energy, feature_grad, grad_radial, grad_mix, grad_out.reshape(CH), grad_shift.reshape(NSPEC)


def solution(mesh):
    sizes = dict(mesh.shape)
    dims = (
        sizes["space"],
        sizes["dp"],
        SPLIT["xh"],
        SPLIT["z"],
        SPLIT["zlo"],
        SPLIT["y"],
        SPLIT["core"],
    )
    return jax.shard_map(
        functools.partial(body, dims),
        mesh=mesh,
        in_specs=(
            P("dp", None, "space"),
            P("dp", None, "space"),
            P("dp", "space"),
            P("dp", "space"),
            P("dp", "space"),
            P("dp", "space"),
            P("dp", "space"),
            P(),
            P(),
            P(),
            P(),
        ),
        out_specs=(P("dp", "space"), P("dp", None, "space"), P(), P(), P(), P()),
        check_vma=False,
    )
```

time: 1190 us -> 88.9 us (0.07)
  waiting for transfers between devices: 692 us -> 0 us
  blocking collectives: 190 us -> 0 us
  starting transfers between devices: 126 us -> 0 us
  loops' own time: 89.5 us -> 0 us
  Pallas kernels: 0 us -> 81.3 us
  local copies, waits for them, and re-layouts: 46.8 us -> 5.99 us
  other arithmetic: 20.6 us -> 0 us
  between operations: 14.3 us -> 1.39 us
    psum x1 -> x0, waiting for transfers between devices: 689 us -> none  [body(): lax.psum((grad_radial, grad_mix, grad_out, grad_shift), ('space', 'dp'))]
    psum x1 -> x0, blocking collectives: 190 us -> none  [body(): lax.psum((grad_radial, grad_mix, grad_out, grad_shift), ('space', 'dp'))]
    ppermute x6 -> x0, starting transfers between devices: 126 us -> none  [the longest x2 104 us: from_behind(): return lax.ppermute(block, axis, route)]
    another operation x42 -> x0, loops' own time: 89.5 us -> none  [the longest x1 26.5 us: pair_pass(): return lax.fori_loop(0, targets.shape[0], visit, totals)]
    pallas_call x0 -> x1, Pallas kernels: none -> 81.3 us  [body(): pl.pallas_call(functools.partial(kernel, dims), out_shape=(jax.ShapeDtype...]
    dynamic_slice x74 -> x0, local copies, waits for them, and re-layouts: 37.4 us -> none  [the longest x20 11.7 us: visit(): scell = sources[index]]
  transfers between devices with their start and end apart: 7 -> 0, of which waited for: 3 -> 0; matrix products, arithmetic and copies ran while one was open for 1% -> 0% of each run, Pallas kernels for 0% -> 0%
where the time goes in v1:
time: 88.9 us; the launch traced here: 88.7 us
  Pallas kernels  81.3 us (91%)
  local copies, waits for them, and re-layouts  5.99 us (7%)
  between operations  1.39 us (2%)
    pallas_call x1, Pallas kernels, body(): pl.pallas_call(functools.partial(kernel, dims), out_shape=(jax.ShapeDtype...  81.3 us
    unnamed x27, local copies, waits for them, and re-layouts  5.99 us

profile of v1, /device:TPU:1, one launch (start us, length us, event | category | flops | bytes accessed | tf_op | source)
XLA Modules:
  0.0 88.7 jit_solution(11931019263893686622)
XLA Ops:
  0.6 0.0 copy-start.9
  1.3 0.0 copy-start.2
  1.3 0.0 copy-done.9
  1.3 0.0 copy-start.3
  1.3 0.0 copy-start.4
  1.3 0.0 copy-start.5
  1.4 0.0 copy-start.6
  1.4 0.0 copy-start.7
  1.4 0.0 copy-start.8
  1.4 0.6 copy-done.2
  2.0 0.0 copy-done.3
  2.0 0.0 copy-done.4
  2.0 0.0 copy-done.5
  2.0 0.0 copy-done.6
  2.0 0.0 copy-done.7
  2.0 0.0 copy-done.8
  2.1 0.0 copy-start
  2.1 0.9 %copy-done = f32[1,128,256]{2,1,0:T(8,128)S(1)} copy-done((f32[1,128,256]{2,1,0:T(8,128)S(1)}, f32[1,128,256]{2,1,0:T(8,128)}, u32[]{:S(2)}) %copy-start) | copy-done | bytes 131096
  3.0 0.0 copy-start.1
  3.0 0.9 %copy-done.1 = bf16[384,128]{1,0:T(8,128)(2,1)S(1)} copy-done((bf16[384,128]{1,0:T(8,128)(2,1)S(1)}, bf16[384,128]{1,0:T(8,128)(2,1)}, u32[]{:S(2)}) %copy-start.1) | copy-done | bytes 98328
  3.9 81.3 %shard_map.154 = (f32[1,256]{1,0:T(1,128)S(1)}, f32[1,128,256]{2,1,0:T(8,128)S(1)}, f32[8,128]{1,0:T(8,128)S(1)}, f32[384,128]{1,0:T(8,128)S(1)}, f32[1,128]{1,0:T(1,128)S(1)}, /*index=5*/f32[1,8]{1,0:T(1,128)S(1)}) custom-call(f32[1,128,256]{2,1,0:T(8,128)S(1)} %copy-done, f32[1,3,256]{2,1,0:T(4,128)S(1)} %copy.17.pos_ref, s32[1,256]{1,0:T(1,128)S(1)} %copy-done.3, ...), custom_call_target="tpu_custom_call" | custom-call | tf_op jit(solution)/shard_map/pallas_call | solution.py:520
  85.1 0.6 copy.25
  85.7 0.7 copy.26
  86.4 0.6 copy.27
  87.0 0.7 copy.28
  87.6 0.5 copy.29
  88.1 0.5 copy.30
  (1 shorter events, 0.0 us)
Async XLA Ops:
  0.6 0.7 copy-start.9
  1.3 0.7 copy-start.2
  1.3 0.7 copy-start.3
  1.3 0.7 copy-start.4
  1.3 0.7 copy-start.5
  1.4 0.7 copy-start.6
  1.4 0.7 copy-start.7
  1.4 0.7 copy-start.8
  2.1 0.9 %copy-start = (f32[1,128,256]{2,1,0:T(8,128)S(1)}, f32[1,128,256]{2,1,0:T(8,128)}, u32[]{:S(2)}) copy-start(f32[1,128,256]{2,1,0:T(8,128)} %feat_ref.1) | copy-start | bytes 393220
  3.0 0.9 %copy-start.1 = (bf16[384,128]{1,0:T(8,128)(2,1)S(1)}, bf16[384,128]{1,0:T(8,128)(2,1)}, u32[]{:S(2)}) copy-start(bf16[384,128]{1,0:T(8,128)(2,1)} %mix_ref.1) | copy-start | bytes 294916

commit v2 on v1

--- a/solution.py
+++ b/solution.py
@@ -44,10 +44,93 @@
     return jnp.transpose(jnp.broadcast_to(row, (BLK, BLK)))
 
 
+def halo_kernel(dims, feat_ref, pos_ref, hfeat_ref, hpos_ref, pos_out, send_sem, recv_sem):
+    nsp = dims[0]
+    sp = lax.axis_index("space")
+    dp = lax.axis_index("dp")
+    has_left = sp > 0
+    has_right = sp < nsp - 1
+    barrier = pltpu.get_barrier_semaphore()
+
+    @pl.when(has_left)
+    def _():
+        pl.semaphore_signal(barrier, inc=1, device_id=(sp - 1, dp), device_id_type=MESH)
+
+    @pl.when(has_right)
+    def _():
+        pl.semaphore_signal(barrier, inc=1, device_id=(sp + 1, dp), device_id_type=MESH)
+
+    for s in range(2):
+        pos_out[s, 0:3, :] = pos_ref[0, :, s * BLK : (s + 1) * BLK]
+        pos_out[s, 3:8, :] = jnp.zeros((5, BLK), F32)
+    pl.semaphore_wait(barrier, has_left.astype(jnp.int32) + has_right.astype(jnp.int32))
+
+    def copies(s, dev):
+        return [
+            pltpu.make_async_remote_copy(
+                src_ref=src,
+                dst_ref=dst,
+                send_sem=send_sem.at[n],
+                recv_sem=recv_sem.at[n],
+                device_id=dev,
+                device_id_type=MESH,
+            )
+            for n, src, dst in (
+                (2 * s, feat_ref.at[0, :, pl.ds(s * BLK, BLK)], hfeat_ref.at[1 - s]),
+                (2 * s + 1, pos_out.at[s], hpos_ref.at[1 - s]),
+            )
+        ]
+
+    to_left = copies(0, (sp - 1, dp))
+    to_right = copies(1, (sp + 1, dp))
+
+    @pl.when(has_left)
+    def _():
+        for copy in to_left:
+            copy.start()
+
+    @pl.when(has_right)
+    def _():
+        for copy in to_right:
+            copy.start()
+
+    @pl.when(has_left)
+    def _():
+        for copy in to_right:
+            copy.wait_recv()
+
+    @pl.when(has_right)
+    def _():
+        for copy in to_left:
+            copy.wait_recv()
+
+    @pl.when(jnp.logical_not(has_left))
+    def _():
+        hfeat_ref[0] = jnp.zeros((CH, BLK), F32)
+        hpos_ref[0] = jnp.zeros((8, BLK), F32)
+
+    @pl.when(jnp.logical_not(has_right))
+    def _():
+        hfeat_ref[1] = jnp.zeros((CH, BLK), F32)
+        hpos_ref[1] = jnp.zeros((8, BLK), F32)
+
+    @pl.when(has_left)
+    def _():
+        for copy in to_left:
+            copy.wait_send()
+
+    @pl.when(has_right)
+    def _():
+        for copy in to_right:
+            copy.wait_send()
+
+
 def kernel(
     dims,
     feat_ref,
     pos_ref,
+    hfeat_ref,
+    hpos_ref,
     spec_ref,
     eg_ref,
     pt_ref,
@@ -74,8 +157,6 @@
     inv,
     racc,
     gext,
-    halo_out,
-    halo_in,
     grad_in,
     big_src,
     big_rs,
@@ -164,18 +245,19 @@
 
     features = feat_ref[0]
     for s in range(2):
-        halo_out[s, 0:CH, :] = features[:, s * BLK : (s + 1) * BLK]
-        halo_out[s, CH : CH + 3, :] = pos_ref[0, :, s * BLK : (s + 1) * BLK]
-        halo_out[s, CH + 3 : CH + 8, :] = jnp.zeros((5, BLK), F32)
         feats[1 + s] = features[:, s * BLK : (s + 1) * BLK]
         for d in range(3):
             scol[1 + s, d] = column(pos_ref[0, d : d + 1, s * BLK : (s + 1) * BLK])
 
+    for h, s in ((0, 0), (1, 3)):
+        feats[s] = hfeat_ref[h]
+        for d in range(3):
+            scol[s, d] = column(hpos_ref[h, d : d + 1, :])
     for b in range(NB):
         wcol[b] = column(w_ref[b : b + 1, :])
-    for s in range(2):
+    for s in range(4):
         for b in range(NB):
-            scaled[1 + s, :, b * BLK : (b + 1) * BLK] = (feats[1 + s] * wcol[b]).astype(BF16)
+            scaled[s, :, b * BLK : (b + 1) * BLK] = (feats[s] * wcol[b]).astype(BF16)
 
     slots = pt_ref.shape[1]
     used = lax.broadcasted_iota(jnp.int32, (1, slots), 1) < pc_ref[...]
@@ -187,8 +269,6 @@
             hit = hit_source & (used & (pt_ref[...] == 2 * t + h))
             cols.append(jnp.sum(jnp.where(hit, 1.0, 0.0), axis=1, keepdims=True))
         live[t] = jnp.where(lane < CELL, cols[0], cols[1])
-
-    msg[...] = jnp.zeros_like(msg)
 
     root3 = math.sqrt(3.0)
     root15 = math.sqrt(15.0)
@@ -238,64 +318,19 @@
                 older, newer = newer, following
             return c
 
-        lax.fori_loop(0, BLK // 16, chunk, 0)
-
-    def forward(p, t, s):
-        produce(p, t, s)
-        msg[t] += nn_dot(scaled[s], table[p])
-
-    forward(1, 0, 1)
-
-    total = plane - 1 + (zlo - 1) + (zhi - 1)
-    total = total + has_left.astype(jnp.int32) + has_right.astype(jnp.int32)
-    total = total + 2 * (me > 0).astype(jnp.int32)
-    pl.semaphore_wait(barrier, total)
-
-    to_left = remote(halo_out.at[0], halo_in.at[1], 0, (sp - 1, dp))
-    to_right = remote(halo_out.at[1], halo_in.at[0], 1, (sp + 1, dp))
-
-    @pl.when(has_left)
-    def _():
-        to_left.start()
-
-    @pl.when(has_right)
-    def _():
-        to_right.start()
-
-    def inner(p, c):
-        forward(p, (p - 1) // 2, 1 + (p - 1) % 2)
+        lax.fori_loop(0, BLK // 16, chunk, 0, unroll=True)
+
+    def forward(p, c):
+        t = p // 3
+        produce(p, t, t + p % 3)
         return c
 
-    lax.fori_loop(2, 5, inner, 0)
-
-    @pl.when(has_left)
-    def _():
-        to_right.wait_recv()
-
-    @pl.when(has_right)
-    def _():
-        to_left.wait_recv()
-
-    @pl.when(jnp.logical_not(has_left))
-    def _():
-        halo_in[0] = jnp.zeros((CH + 8, BLK), F32)
-
-    @pl.when(jnp.logical_not(has_right))
-    def _():
-        halo_in[1] = jnp.zeros((CH + 8, BLK), F32)
-
-    for h, s in ((0, 0), (1, 3)):
-        feats[s] = halo_in[h, 0:CH, :]
-        for d in range(3):
-            scol[s, d] = column(halo_in[h, CH + d : CH + d + 1, :])
-        for b in range(NB):
-            scaled[s, :, b * BLK : (b + 1) * BLK] = (feats[s] * wcol[b]).astype(BF16)
-
-    def outer(h, c):
-        forward(5 * h, h, 3 * h)
-        return c
-
-    lax.fori_loop(0, 2, outer, 0)
+    lax.fori_loop(0, 6, forward, 0)
+    for t in range(2):
+        total = nn_dot(scaled[t], table[3 * t])
+        for k in range(1, 3):
+            total += nn_dot(scaled[t + k], table[3 * t + k])
+        msg[t] = total
 
     mix = mix_ref[...]
     mix_t = jnp.concatenate(
@@ -367,6 +402,11 @@
         copies = remote(part, part, n, dev)
         return copies
 
+    total = plane - 1 + (zlo - 1) + (zhi - 1)
+    total = total + has_left.astype(jnp.int32) + has_right.astype(jnp.int32)
+    total = total + 2 * (me > 0).astype(jnp.int32)
+    pl.semaphore_wait(barrier, total)
+
     big_rs[me] = big_src[me]
     send_plane(lambda g: big_src.at[g], big_rs.at[me], 2)
 
@@ -387,7 +427,7 @@
             gext[s] = add
             return c
 
-        lax.fori_loop(0, NB // 2, step, 0)
+        lax.fori_loop(0, NB // 2, step, 0, unroll=True)
 
     gext[0] = jnp.zeros((CH, BLK), F32)
     gext[3] = jnp.zeros((CH, BLK), F32)
@@ -477,12 +517,10 @@
 
     @pl.when(has_left)
     def _():
-        to_left.wait_send()
         back_left.wait_send()
 
     @pl.when(has_right)
     def _():
-        to_right.wait_send()
         back_right.wait_send()
 
     @pl.when(me > 0)
@@ -517,6 +555,21 @@
     per = ROWS // plane
     atoms = 2 * BLK
     vmem = pl.BlockSpec(memory_space=pltpu.VMEM)
+    halo_features, halo_positions = pl.pallas_call(
+        functools.partial(halo_kernel, dims),
+        out_shape=(
+            jax.ShapeDtypeStruct((2, CH, BLK), F32),
+            jax.ShapeDtypeStruct((2, 8, BLK), F32),
+        ),
+        in_specs=[vmem] * 2,
+        out_specs=(vmem,) * 2,
+        scratch_shapes=[
+            pltpu.VMEM((2, 8, BLK), F32),
+            pltpu.SemaphoreType.DMA((4,)),
+            pltpu.SemaphoreType.DMA((4,)),
+        ],
+        compiler_params=pltpu.CompilerParams(collective_id=1, has_side_effects=True),
+    )(node_features, positions)
     outs = pl.pallas_call(
         functools.partial(kernel, dims),
         out_shape=(
@@ -527,7 +580,7 @@
             jax.ShapeDtypeStruct((1, CH), F32),
             jax.ShapeDtypeStruct((1, NSPEC), F32),
         ),
-        in_specs=[vmem] * 11,
+        in_specs=[vmem] * 13,
         out_specs=(vmem,) * 6,
         scratch_shapes=[
             pltpu.VMEM((6, NB * BLK, NY * BLK), BF16),
@@ -541,8 +594,6 @@
             pltpu.VMEM((3 * CH, atoms), BF16),
             pltpu.VMEM((NB, CH, BLK), F32),
             pltpu.VMEM((4, CH, BLK), F32),
-            pltpu.VMEM((2, CH + 8, BLK), F32),
-            pltpu.VMEM((2, CH + 8, BLK), F32),
             pltpu.VMEM((2, CH, BLK), F32),
             pltpu.VMEM((plane, per, CH), F32),
             pltpu.VMEM((plane, per, CH), F32),
@@ -565,6 +616,8 @@
     )(
         node_features,
         positions,
+        halo_features,
+        halo_positions,
         species,
         energy_cotangent,
         pair_target,

time: 88.9 us -> 90.1 us (1.013)
  local copies, waits for them, and re-layouts: 5.99 us -> 7.95 us
  Pallas kernels: 81.3 us -> 80.3 us
    pallas_call x1, Pallas kernels: 81.3 us -> 62.3 us  [body(): pl.pallas_call(functools.partial(kernel, dims), out_shape=(jax.ShapeDtype...]
    pallas_call x0 -> x1, Pallas kernels: none -> 18 us  [body(): pl.pallas_call(functools.partial(halo_kernel, dims), out_shape=(jax.Shape...]
    unnamed x27 -> x31, local copies, waits for them, and re-layouts: 5.99 us -> 7.95 us
where the time goes in v2:
time: 90.1 us; the launch traced here: 89.7 us
  Pallas kernels  80.3 us (89%)
  local copies, waits for them, and re-layouts  7.95 us (9%)
  between operations  1.42 us (2%)
    pallas_call x1, Pallas kernels, body(): pl.pallas_call(functools.partial(kernel, dims), out_shape=(jax.ShapeDtype...  62.3 us
    pallas_call x1, Pallas kernels, body(): pl.pallas_call(functools.partial(halo_kernel, dims), out_shape=(jax.Shape...  18 us
    unnamed x31, local copies, waits for them, and re-layouts  7.95 us

profile of v2, /device:TPU:1, one launch (start us, length us, event | category | flops | bytes accessed | tf_op | source)
XLA Modules:
  0.0 89.7 jit_solution(10904669223689899276)
XLA Ops:
  0.6 0.0 copy-start
  1.3 1.3 %copy.18.pos_ref = f32[1,3,256]{2,1,0:T(4,128)} copy(f32[1,3,256]{2,0,1:T(1,128)} %param.12) | data formatting | bytes 6144 | tf_op args[1]
  2.6 0.0 copy-start.3
  2.6 0.0 copy-start.5
  2.6 0.0 copy-start.11
  2.6 18.0 %shard_map.154 = (f32[2,128,128]{2,1,0:T(8,128)}, f32[2,8,128]{2,1,0:T(8,128)}) custom-call(f32[1,128,256]{2,1,0:T(8,128)} %feat_ref.3, f32[1,3,256]{2,1,0:T(4,128)} %copy.18.pos_ref), custom_call_target="tpu_custom_call" | custom-call | tf_op jit(solution)/shard_map/pallas_call | solution.py:558
  20.6 0.0 copy-start.7
  20.6 0.0 copy-start.9
  20.6 0.0 copy-start.10
  20.7 0.0 copy-start.6
  20.7 0.0 copy-start.8
  20.7 0.0 copy-done
  20.7 0.0 copy-done.3
  20.7 0.0 copy-done.5
  20.7 0.0 copy-done.11
  20.7 0.6 copy-done.7
  21.3 0.0 copy-done.9
  21.3 0.0 copy-done.10
  21.3 0.0 copy-done.6
  21.4 0.0 copy-done.8
  21.4 0.0 copy-start.1
  21.4 0.9 %copy-done.1 = f32[2,128,128]{2,1,0:T(8,128)S(1)} copy-done((f32[2,128,128]{2,1,0:T(8,128)S(1)}, f32[2,128,128]{2,1,0:T(8,128)}, u32[]{:S(2)}) %copy-start.1) | copy-done | bytes 131096
  22.3 0.0 copy-start.2
  22.3 0.9 copy-done.2
  23.2 0.0 copy-start.4
  23.2 0.7 copy-done.4
  23.9 62.3 %shard_map.155 = (f32[1,256]{1,0:T(1,128)S(1)}, f32[1,128,256]{2,1,0:T(8,128)S(1)}, f32[8,128]{1,0:T(8,128)S(1)}, f32[384,128]{1,0:T(8,128)S(1)}, f32[1,128]{1,0:T(1,128)S(1)}, /*index=5*/f32[1,8]{1,0:T(1,128)S(1)}) custom-call(f32[1,128,256]{2,1,0:T(8,128)S(1)} %copy-done, f32[1,3,256]{2,1,0:T(4,128)S(1)} %copy-done.3, f32[2,128,128]{2,1,0:T(8,128)S(1)} %copy-done.1, ...), custom_call_target="tpu_custom_call" | custom-call | tf_op jit(solution)/shard_map/pallas_call | solution.py:573
  86.2 0.6 copy.26
  86.8 0.7 copy.27
  87.4 0.6 copy.28
  88.0 0.7 copy.29
  88.7 0.5 copy.30
  89.2 0.5 copy.31
Async XLA Ops:
  0.6 20.1 %copy-start = (f32[1,128,256]{2,1,0:T(8,128)S(1)}, f32[1,128,256]{2,1,0:T(8,128)}, u32[]{:S(2)}) copy-start(f32[1,128,256]{2,1,0:T(8,128)} %feat_ref.3) | copy-start | bytes 393220
  2.6 18.1 %copy-start.3 = (f32[1,3,256]{2,1,0:T(4,128)S(1)}, f32[1,3,256]{2,1,0:T(4,128)}, u32[]{:S(2)}) copy-start(f32[1,3,256]{2,1,0:T(4,128)} %copy.18.pos_ref) | copy-start | bytes 9220
  2.6 18.1 %copy-start.5 = (f32[8,128]{1,0:T(8,128)S(1)}, f32[8,128]{1,0:T(8,128)}, u32[]{:S(2)}) copy-start(f32[8,128]{1,0:T(8,128)} %w_ref.1) | copy-start | bytes 12292
  2.6 18.1 %copy-start.11 = (f32[8]{0:T(128)S(1)}, f32[8]{0:T(128)}, u32[]{:S(2)}) copy-start(f32[8]{0:T(128)} %param.21) | copy-start | bytes 100
  20.6 0.7 copy-start.7
  20.6 0.7 copy-start.9
  20.6 0.7 copy-start.10
  20.7 0.7 copy-start.6
  20.7 0.7 copy-start.8
  21.4 0.9 %copy-start.1 = (f32[2,128,128]{2,1,0:T(8,128)S(1)}, f32[2,128,128]{2,1,0:T(8,128)}, u32[]{:S(2)}) copy-start(f32[2,128,128]{2,1,0:T(8,128)} %get-tuple-element.14.hfeat_ref) | copy-start | bytes 393220
  22.3 0.9 copy-start.2
  23.2 0.7 copy-start.4

commit v3 on v1

--- a/solution.py
+++ b/solution.py
@@ -19,7 +19,6 @@
 MESH = pl.DeviceIdType.MESH
 
 SPLIT = {"xh": 2, "z": 32, "zlo": 4, "y": 4, "core": 2}
-ROWS = 512
 
 COS_TERMS = [(-1.0) ** k * math.pi ** (2 * k) / math.factorial(2 * k) for k in range(11)]
 SINC_TERMS = [(-1.0) ** k * math.pi ** (2 * k) / math.factorial(2 * k + 1) for k in range(10)]
@@ -44,8 +43,62 @@
     return jnp.transpose(jnp.broadcast_to(row, (BLK, BLK)))
 
 
+def store_all(*refs):
+    sources, targets, sem = refs[:6], refs[6:12], refs[12]
+    copies = [pltpu.make_async_copy(s, t, sem.at[n]) for n, (s, t) in enumerate(zip(sources, targets))]
+    for copy in copies:
+        copy.start()
+    for copy in copies:
+        copy.wait()
+
+
 def kernel(
     dims,
+    feat_hbm,
+    pos_hbm,
+    spec_hbm,
+    eg_hbm,
+    pt_hbm,
+    ps_hbm,
+    pc_hbm,
+    w_hbm,
+    mix_hbm,
+    ro_hbm,
+    sh_hbm,
+    energy_hbm,
+    fgrad_hbm,
+    rad_hbm,
+    mixg_hbm,
+    rog_hbm,
+    shg_hbm,
+    table,
+    scaled,
+    feats,
+    scol,
+    wcol,
+    live,
+    msg,
+    gmsg,
+    inv,
+    upd,
+    gpre,
+    racc,
+    gext,
+    halo_out,
+    halo_in,
+    grad_in,
+    big_src,
+    big_rs,
+    z_a,
+    z_b,
+    z_as,
+    z_bs,
+    big_ag,
+    sm_src,
+    sm_pl,
+    sm_sum,
+    sm_x,
+    sm_z,
     feat_ref,
     pos_ref,
     spec_ref,
@@ -63,32 +116,8 @@
     mixg_ref,
     rog_ref,
     shg_ref,
-    table,
-    scaled,
-    feats,
-    scol,
-    wcol,
-    live,
-    msg,
-    gmsg,
-    inv,
-    racc,
-    gext,
-    halo_out,
-    halo_in,
-    grad_in,
-    big_src,
-    big_rs,
-    z_a,
-    z_b,
-    z_as,
-    z_bs,
-    big_ag,
-    sm_src,
-    sm_pl,
-    sm_sum,
-    sm_x,
-    sm_z,
+    in_sem,
+    out_sem,
     send_sem,
     recv_sem,
 ):
@@ -131,6 +160,40 @@
             device_id_type=MESH,
         )
 
+    fetches = [
+        pltpu.make_async_copy(src, dst, in_sem.at[n])
+        for n, (src, dst) in enumerate(
+            (
+                (feat_hbm, feat_ref),
+                (pos_hbm, pos_ref),
+                (pt_hbm, pt_ref),
+                (ps_hbm, ps_ref),
+                (pc_hbm, pc_ref),
+                (w_hbm, w_ref),
+                (eg_hbm, eg_ref),
+                (spec_hbm, spec_ref),
+                (mix_hbm, mix_ref),
+                (ro_hbm, ro_ref),
+                (sh_hbm, sh_ref),
+            )
+        )
+    ]
+    for fetch in fetches:
+        fetch.start()
+    stores = [
+        pltpu.make_async_copy(src, dst, out_sem.at[n])
+        for n, (src, dst) in enumerate(
+            (
+                (energy_ref, energy_hbm),
+                (fgrad_ref, fgrad_hbm),
+                (rad_ref, rad_hbm),
+                (mixg_ref, mixg_hbm),
+                (rog_ref, rog_hbm),
+                (shg_ref, shg_hbm),
+            )
+        )
+    ]
+
     barrier = pltpu.get_barrier_semaphore()
 
     def greet(dev):
@@ -162,14 +225,17 @@
         greet(at_z((zz + me) % nz))
         greet(at_z((zz + nz - me) % nz))
 
+    for fetch in fetches[:6]:
+        fetch.wait()
     features = feat_ref[0]
     for s in range(2):
         halo_out[s, 0:CH, :] = features[:, s * BLK : (s + 1) * BLK]
-        halo_out[s, CH : CH + 3, :] = pos_ref[0, :, s * BLK : (s + 1) * BLK]
+        for d in range(3):
+            halo_out[s, CH + d : CH + d + 1, :] = pos_ref[d, :, s * BLK : (s + 1) * BLK]
         halo_out[s, CH + 3 : CH + 8, :] = jnp.zeros((5, BLK), F32)
         feats[1 + s] = features[:, s * BLK : (s + 1) * BLK]
         for d in range(3):
-            scol[1 + s, d] = column(pos_ref[0, d : d + 1, s * BLK : (s + 1) * BLK])
+            scol[1 + s, d] = column(pos_ref[d, :, s * BLK : (s + 1) * BLK])
 
     for b in range(NB):
         wcol[b] = column(w_ref[b : b + 1, :])
@@ -198,7 +264,7 @@
 
     def produce(p, t, s):
         lanes = pl.ds(pl.multiple_of(t * BLK, BLK), BLK)
-        targets = [jnp.broadcast_to(pos_ref[0, d : d + 1, lanes], (16, BLK)) for d in range(3)]
+        targets = [jnp.broadcast_to(pos_ref[d, :, lanes], (16, BLK)) for d in range(3)]
         shift = jnp.where(s == t + 1, 0, 2 * BLK)
 
         def chunk(q, c):
@@ -238,7 +304,7 @@
                 older, newer = newer, following
             return c
 
-        lax.fori_loop(0, BLK // 16, chunk, 0)
+        lax.fori_loop(0, BLK // 16, chunk, 0, unroll=True)
 
     def forward(p, t, s):
         produce(p, t, s)
@@ -297,14 +363,13 @@
 
     lax.fori_loop(0, 2, outer, 0)
 
+    for fetch in fetches[6:]:
+        fetch.wait()
     mix = mix_ref[...]
     mix_t = jnp.concatenate(
         [jnp.transpose(mix[k * CH : (k + 1) * CH].astype(F32)) for k in range(3)], axis=1
     ).astype(BF16)
     ro_col = column(ro_ref[...])
-    lane_ch = lax.broadcasted_iota(jnp.int32, (CH, BLK), 1)
-    row_sp = lax.broadcasted_iota(jnp.int32, (NSPEC, BLK), 0)
-    shift_col = jnp.transpose(jnp.broadcast_to(sh_ref[...], (NSPEC, NSPEC)))[:, 0:1]
     for t in range(2):
         lanes = slice(t * BLK, (t + 1) * BLK)
         inv[0:CH, lanes] = msg[t, :, 0:BLK].astype(BF16)
@@ -314,27 +379,54 @@
                 m = msg[t, :, y * BLK : (y + 1) * BLK]
                 acc = m * m if acc is None else acc + m * m
             inv[k * CH : (k + 1) * CH, lanes] = (0.5 * acc).astype(BF16)
-    mixg = jnp.zeros((3 * CH, CH), F32)
+    row_sp = lax.broadcasted_iota(jnp.int32, (NSPEC, BLK), 0)
     rog = jnp.zeros((CH, BLK), F32)
     shg = jnp.zeros((NSPEC, BLK), F32)
     for t in range(2):
         lanes = slice(t * BLK, (t + 1) * BLK)
-        invariants = inv[:, lanes]
-        preact = nn_dot(mix_t, invariants)
+        preact = nn_dot(mix_t, inv[:, lanes])
         gate = 1.0 / (1.0 + jnp.exp(-preact))
         updated = feats[1 + t] + preact * gate
         eg = eg_ref[:, lanes]
+        rog += updated * eg
+        shg += (spec_ref[:, lanes] == row_sp).astype(F32) * eg
+        base = eg * ro_col
+        upd[t] = updated
+        gext[1 + t] = base
+        gpre[:, lanes] = (base * gate * (1.0 + preact * (1.0 - gate))).astype(BF16)
+
+    per = 3 * CH // plane
+    mixg = nt_dot(inv[...], gpre[...])
+    rog = jnp.sum(jnp.transpose(rog), axis=0, keepdims=True)
+    shg = jnp.concatenate([shg, jnp.zeros((CH - NSPEC, BLK), F32)], axis=0)
+    shg = jnp.sum(jnp.transpose(shg), axis=0, keepdims=True)
+    for g in range(plane):
+        big_src[g, 0:per, :] = mixg[g * per : (g + 1) * per]
+        big_src[g, per : per + 1, :] = (rog, shg, jnp.zeros((1, BLK), F32))[min(g, 2)]
+
+    def send_plane(src, dst, n):
+        def step(k, c):
+            g = plane_peer(k)
+            remote(src(g), dst, n, at_plane(g)).start()
+            return c
+
+        lax.fori_loop(1, plane, step, 0)
+
+    def wait_slots(buf, n, count, dev):
+        part = buf.at[pl.ds(0, count)]
+        return remote(part, part, n, dev)
+
+    big_rs[me] = big_src[me]
+    send_plane(lambda g: big_src.at[g], big_rs.at[me], 2)
+
+    shift_col = jnp.transpose(jnp.broadcast_to(sh_ref[...], (NSPEC, NSPEC)))[:, 0:1]
+    for t in range(2):
+        lanes = slice(t * BLK, (t + 1) * BLK)
         onehot = (spec_ref[:, lanes] == row_sp).astype(F32)
-        energy_ref[:, lanes] = jnp.sum(updated * ro_col, axis=0, keepdims=True) + jnp.sum(
+        energy_ref[:, lanes] = jnp.sum(upd[t] * ro_col, axis=0, keepdims=True) + jnp.sum(
             onehot * shift_col, axis=0, keepdims=True
         )
-        rog += updated * eg
-        shg += onehot * eg
-        base = eg * ro_col
-        gext[1 + t] = base
-        gpre = (base * gate * (1.0 + preact * (1.0 - gate))).astype(BF16)
-        mixg += nt_dot(invariants, gpre)
-        ginv = nn_dot(mix, gpre)
+        ginv = nn_dot(mix, gpre[:, lanes])
         gmsg[t, :, 0:BLK] = ginv[0:CH].astype(BF16)
         for y in range(1, NY):
             k = 1 if y < 4 else 2
@@ -342,33 +434,7 @@
                 ginv[k * CH : (k + 1) * CH] * msg[t, :, y * BLK : (y + 1) * BLK]
             ).astype(BF16)
 
-    per = ROWS // plane
-    tail = jnp.concatenate(
-        [
-            jnp.sum(jnp.transpose(rog), axis=0, keepdims=True),
-            jnp.zeros((7, BLK), F32),
-            jnp.sum(jnp.transpose(jnp.concatenate([shg, jnp.zeros((CH - NSPEC, BLK), F32)], axis=0)), axis=0, keepdims=True),
-            jnp.zeros((ROWS - 3 * CH - 9, BLK), F32),
-        ],
-        axis=0,
-    )
-    big_src[...] = jnp.concatenate([mixg, tail], axis=0).reshape(plane, per, CH)
-
-    def send_plane(src, dst, n):
-        def step(k, c):
-            g = plane_peer(k)
-            remote(src(g), dst, n, at_plane(g)).start()
-            return c
-
-        lax.fori_loop(1, plane, step, 0)
-
-    def wait_slots(buf, n, count, dev):
-        part = buf.at[pl.ds(0, count)]
-        copies = remote(part, part, n, dev)
-        return copies
-
-    big_rs[me] = big_src[me]
-    send_plane(lambda g: big_src.at[g], big_rs.at[me], 2)
+    stores[0].start()
 
     racc[...] = jnp.zeros_like(racc)
 
@@ -387,7 +453,7 @@
             gext[s] = add
             return c
 
-        lax.fori_loop(0, NB // 2, step, 0)
+        lax.fori_loop(0, NB // 2, step, 0, unroll=True)
 
     gext[0] = jnp.zeros((CH, BLK), F32)
     gext[3] = jnp.zeros((CH, BLK), F32)
@@ -408,6 +474,15 @@
     any_plane = at_plane(plane_peer(1))
     any_a = at_z(za_peer(1))
     any_b = at_z(zb_peer(1))
+
+    backward(1, [(1, 0), (3, 1)])
+    backward(2, [(2, 0), (4, 1)])
+
+    sm_src[...] = jnp.concatenate(
+        [jnp.sum(jnp.transpose(racc[b]), axis=0, keepdims=True) for b in range(NB)], axis=0
+    )
+    sm_pl[me] = sm_src[...]
+    send_plane(lambda g: sm_src, sm_pl.at[me], 7)
 
     wait_slots(big_rs, 2, plane - 1, any_plane).wait_recv()
     z_as[...] = jnp.sum(big_rs[...], axis=0)
@@ -415,26 +490,12 @@
     for k in range(1, zlo):
         remote(z_as, z_a.at[zz % zlo], 5, at_z(za_peer(k))).start()
 
-    backward(1, [(1, 0), (3, 1)])
-
     wait_slots(z_a, 5, zlo - 1, any_a).wait_recv()
     z_bs[...] = jnp.sum(z_a[...], axis=0)
     z_b[zz // zlo] = z_bs[...]
     for k in range(1, zhi):
         remote(z_bs, z_b.at[zz // zlo], 6, at_z(zb_peer(k))).start()
 
-    backward(2, [(2, 0), (4, 1)])
-
-    sm_src[...] = jnp.concatenate(
-        [jnp.sum(jnp.transpose(racc[b]), axis=0, keepdims=True) for b in range(NB)], axis=0
-    )
-    sm_pl[me] = sm_src[...]
-    send_plane(lambda g: sm_src, sm_pl.at[me], 7)
-
-    wait_slots(z_b, 6, zhi - 1, any_b).wait_recv()
-    big_ag[me] = jnp.sum(z_b[...], axis=0)
-    send_plane(lambda g: big_ag.at[me], big_ag.at[me], 8)
-
     wait_slots(sm_pl, 7, plane - 1, any_plane).wait_recv()
     sm_sum[...] = jnp.sum(sm_pl[...], axis=0)
     slot = (zz + me) % nz
@@ -443,6 +504,23 @@
     @pl.when(me > 0)
     def _():
         to_z.start()
+
+    @pl.when(has_left)
+    def _():
+        back_right.wait_recv()
+        gext[1] += grad_in[0]
+
+    @pl.when(has_right)
+    def _():
+        back_left.wait_recv()
+        gext[2] += grad_in[1]
+
+    for t in range(2):
+        fgrad_ref[0, :, t * BLK : (t + 1) * BLK] = gext[1 + t]
+    stores[1].start()
+
+    @pl.when(me > 0)
+    def _():
         to_z.wait_recv()
 
     @pl.when(me == 0)
@@ -452,28 +530,24 @@
     sm_z[slot] = sm_x[...]
     send_plane(lambda g: sm_x, sm_z.at[slot], 10)
 
-    @pl.when(has_left)
-    def _():
-        back_right.wait_recv()
-        gext[1] += grad_in[0]
-
-    @pl.when(has_right)
-    def _():
-        back_left.wait_recv()
-        gext[2] += grad_in[1]
-
-    for t in range(2):
-        fgrad_ref[0, :, t * BLK : (t + 1) * BLK] = gext[1 + t]
+    wait_slots(z_b, 6, zhi - 1, any_b).wait_recv()
+    big_ag[me] = jnp.sum(z_b[...], axis=0)
+    send_plane(lambda g: big_ag.at[me], big_ag.at[me], 8)
 
     scale = 1.0 / math.sqrt(2 * BLK * nsp * ndp)
     wait_slots(big_ag, 8, plane - 1, any_plane).wait_recv()
-    whole = big_ag[...].reshape(ROWS, CH) * scale
-    mixg_ref[...] = whole[0 : 3 * CH]
-    rog_ref[...] = whole[3 * CH : 3 * CH + 1]
-    shg_ref[...] = whole[3 * CH + 8 : 3 * CH + 9, 0:NSPEC]
+    for g in range(plane):
+        mixg_ref[g * per : (g + 1) * per, :] = big_ag[g, 0:per, :] * scale
+    rog_ref[...] = big_ag[0, per : per + 1, :] * scale
+    shg_ref[...] = big_ag[1, per : per + 1, 0:NSPEC] * scale
+    for store in stores[3:]:
+        store.start()
 
     wait_slots(sm_z, 10, plane - 1, any_plane).wait_recv()
     rad_ref[...] = jnp.sum(sm_z[...], axis=0) * scale
+    stores[2].start()
+    for store in stores:
+        store.wait()
 
     @pl.when(has_left)
     def _():
@@ -514,21 +588,22 @@
     nsp, ndp, nxh, nz, zlo, ny, nco = dims
     plane = nxh * ndp * ny * nco
     zhi = nz // zlo
-    per = ROWS // plane
+    per = 3 * CH // plane + 1
     atoms = 2 * BLK
-    vmem = pl.BlockSpec(memory_space=pltpu.VMEM)
+    hbm = pl.BlockSpec(memory_space=pltpu.HBM)
+    shapes = (
+        jax.ShapeDtypeStruct((1, atoms), F32),
+        jax.ShapeDtypeStruct((1, CH, atoms), F32),
+        jax.ShapeDtypeStruct((NB, CH), F32),
+        jax.ShapeDtypeStruct((3 * CH, CH), F32),
+        jax.ShapeDtypeStruct((1, CH), F32),
+        jax.ShapeDtypeStruct((1, NSPEC), F32),
+    )
     outs = pl.pallas_call(
         functools.partial(kernel, dims),
-        out_shape=(
-            jax.ShapeDtypeStruct((1, atoms), F32),
-            jax.ShapeDtypeStruct((1, CH, atoms), F32),
-            jax.ShapeDtypeStruct((NB, CH), F32),
-            jax.ShapeDtypeStruct((3 * CH, CH), F32),
-            jax.ShapeDtypeStruct((1, CH), F32),
-            jax.ShapeDtypeStruct((1, NSPEC), F32),
-        ),
-        in_specs=[vmem] * 11,
-        out_specs=(vmem,) * 6,
+        out_shape=shapes,
+        in_specs=[hbm] * 11,
+        out_specs=(hbm,) * 6,
         scratch_shapes=[
             pltpu.VMEM((6, NB * BLK, NY * BLK), BF16),
             pltpu.VMEM((4, CH, NB * BLK), BF16),
@@ -539,6 +614,8 @@
             pltpu.VMEM((2, CH, NY * BLK), F32),
             pltpu.VMEM((2, CH, NY * BLK), BF16),
             pltpu.VMEM((3 * CH, atoms), BF16),
+            pltpu.VMEM((2, CH, BLK), F32),
+            pltpu.VMEM((CH, atoms), BF16),
             pltpu.VMEM((NB, CH, BLK), F32),
             pltpu.VMEM((4, CH, BLK), F32),
             pltpu.VMEM((2, CH + 8, BLK), F32),
@@ -556,15 +633,29 @@
             pltpu.VMEM((NB, CH), F32),
             pltpu.VMEM((NB, CH), F32),
             pltpu.VMEM((nz, NB, CH), F32),
+            pltpu.VMEM((1, CH, atoms), F32),
+            pltpu.VMEM((3, 1, atoms), F32),
+            pltpu.VMEM((1, atoms), jnp.int32),
+            pltpu.VMEM((1, atoms), F32),
+            pltpu.VMEM(pair_target.shape, jnp.int32),
+            pltpu.VMEM(pair_target.shape, jnp.int32),
+            pltpu.VMEM((1, 1), jnp.int32),
+            pltpu.VMEM((NB, CH), F32),
+            pltpu.VMEM((3 * CH, CH), BF16),
+            pltpu.VMEM((1, CH), F32),
+            pltpu.VMEM((1, NSPEC), F32),
+            *(pltpu.VMEM(s.shape, s.dtype) for s in shapes),
+            pltpu.SemaphoreType.DMA((11,)),
+            pltpu.SemaphoreType.DMA((6,)),
             pltpu.SemaphoreType.DMA((11,)),
             pltpu.SemaphoreType.DMA((11,)),
         ],
         compiler_params=pltpu.CompilerParams(
-            collective_id=0, has_side_effects=True, vmem_limit_bytes=48 << 20
+            collective_id=0, has_side_effects=True, vmem_limit_bytes=64 << 20
         ),
     )(
         node_features,
-        positions,
+        jnp.transpose(positions, (1, 0, 2)),
         species,
         energy_cotangent,
         pair_target,
@@ -575,7 +666,14 @@
         readout_weight.reshape(1, CH),
         species_shift.reshape(1, NSPEC),
     )
-    energy, feature_grad, grad_radial, grad_mix, grad_out, grad_shift = outs
+    energy, feature_grad, grad_radial, grad_mix, grad_out, grad_shift = pl.pallas_call(
+        store_all,
+        out_shape=shapes,
+        in_specs=[pl.BlockSpec(memory_space=pltpu.VMEM)] * 6,
+        out_specs=(hbm,) * 6,
+        scratch_shapes=[pltpu.SemaphoreType.DMA((6,))],
+        compiler_params=pltpu.CompilerParams(vmem_limit_bytes=64 << 20),
+    )(*outs)
     return energy, feature_grad, grad_radial, grad_mix, grad_out.reshape(CH), grad_shift.reshape(NSPEC)
 
 

time: 88.9 us -> 70.4 us (0.79)
  Pallas kernels: 81.3 us -> 69 us
  local copies, waits for them, and re-layouts: 5.99 us -> 0 us
    pallas_call x1 -> x2, Pallas kernels: 81.3 us -> 69 us  [the longest x1 67.2 us: body(): pl.pallas_call(functools.partial(kernel, dims), out_shape=shapes, in_spec...]
    unnamed x27 -> x0, local copies, waits for them, and re-layouts: 5.99 us -> none
where the time goes in v3:
time: 70.4 us; the launch traced here: 70.3 us
  Pallas kernels  69 us (98%)
  between operations  1.29 us (2%)
    pallas_call x1, Pallas kernels, body(): pl.pallas_call(functools.partial(kernel, dims), out_shape=shapes, in_spec...  67.2 us
    pallas_call x1, Pallas kernels, body(): pl.pallas_call(store_all, out_shape=shapes, in_specs=[pl.BlockSpec(memory...  1.78 us

profile of v3, /device:TPU:1, one launch (start us, length us, event | category | flops | bytes accessed | tf_op | source)
XLA Modules:
  0.0 70.3 jit_solution(3662086270501001244)
XLA Ops:
  1.3 67.2 %shard_map.154 = (f32[1,256]{1,0:T(1,128)}, f32[1,128,256]{2,1,0:T(8,128)}, f32[8,128]{1,0:T(8,128)}, f32[384,128]{1,0:T(8,128)}, f32[1,128]{1,0:T(1,128)}, /*index=5*/f32[1,8]{1,0:T(1,128)}) custom-call(f32[1,128,256]{2,1,0:T(8,128)} %feat_hbm.1, f32[3,1,256]{2,1,0:T(1,128)} %bitcast.5, s32[1,256]{1,0:T(1,128)} %spec_hbm.1, f32[1,256]{1,0:T(1,128)} %eg_hbm.1, ...), custom_call_target="tpu_custom_call" | custom-call | tf_op jit(solution)/shard_map/pallas_call | solution.py:602
  68.5 1.8 %shard_map.155 = (f32[1,256]{1,0:T(1,128)}, f32[1,128,256]{2,1,0:T(8,128)}, f32[8,128]{1,0:T(8,128)}, f32[384,128]{1,0:T(8,128)}, f32[1,128]{1,0:T(1,128)}, /*index=5*/f32[1,8]{1,0:T(1,128)}) custom-call(f32[1,256]{1,0:T(1,128)} %get-tuple-element.18.refs_0_, f32[1,128,256]{2,1,0:T(8,128)} %get-tuple-element.19.refs_1_, f32[8,128]{1,0:T(8,128)} %get-tuple-element.20.refs_2_, ...), custom_call_target="tpu_custom_call" | custom-call | tf_op jit(solution)/shard_map/pallas_call | solution.py:669

commit v4 on v3

--- a/solution.py
+++ b/solution.py
@@ -80,6 +80,8 @@
     msg,
     gmsg,
     inv,
+    mixt,
+    roc,
     upd,
     gpre,
     racc,
@@ -312,6 +314,13 @@
 
     forward(1, 0, 1)
 
+    for fetch in fetches[6:]:
+        fetch.wait()
+    for k in range(3):
+        rows = slice(k * CH, (k + 1) * CH)
+        mixt[:, rows] = jnp.transpose(mix_ref[rows, :].astype(F32)).astype(BF16)
+    roc[...] = column(ro_ref[...])
+
     total = plane - 1 + (zlo - 1) + (zhi - 1)
     total = total + has_left.astype(jnp.int32) + has_right.astype(jnp.int32)
     total = total + 2 * (me > 0).astype(jnp.int32)
@@ -363,13 +372,9 @@
 
     lax.fori_loop(0, 2, outer, 0)
 
-    for fetch in fetches[6:]:
-        fetch.wait()
     mix = mix_ref[...]
-    mix_t = jnp.concatenate(
-        [jnp.transpose(mix[k * CH : (k + 1) * CH].astype(F32)) for k in range(3)], axis=1
-    ).astype(BF16)
-    ro_col = column(ro_ref[...])
+    mix_t = mixt[...]
+    ro_col = roc[...]
     for t in range(2):
         lanes = slice(t * BLK, (t + 1) * BLK)
         inv[0:CH, lanes] = msg[t, :, 0:BLK].astype(BF16)
@@ -614,6 +619,8 @@
             pltpu.VMEM((2, CH, NY * BLK), F32),
             pltpu.VMEM((2, CH, NY * BLK), BF16),
             pltpu.VMEM((3 * CH, atoms), BF16),
+            pltpu.VMEM((CH, 3 * CH), BF16),
+            pltpu.VMEM((CH, BLK), F32),
             pltpu.VMEM((2, CH, BLK), F32),
             pltpu.VMEM((CH, atoms), BF16),
             pltpu.VMEM((NB, CH, BLK), F32),

time: 70.4 us -> 70.4 us (level)
  no operation moved by 1% of the time
where the time goes in v4:
time: 70.4 us; the launch traced here: 70.2 us
  Pallas kernels  69 us (98%)
  between operations  1.29 us (2%)
    pallas_call x1, Pallas kernels, body(): pl.pallas_call(functools.partial(kernel, dims), out_shape=shapes, in_spec...  67.2 us
    pallas_call x1, Pallas kernels, body(): pl.pallas_call(store_all, out_shape=shapes, in_specs=[pl.BlockSpec(memory...  1.78 us

profile of v4, /device:TPU:1, one launch (start us, length us, event | category | flops | bytes accessed | tf_op | source)
XLA Modules:
  0.0 70.2 jit_solution(893166126517638581)
XLA Ops:
  1.3 67.2 %shard_map.154 = (f32[1,256]{1,0:T(1,128)}, f32[1,128,256]{2,1,0:T(8,128)}, f32[8,128]{1,0:T(8,128)}, f32[384,128]{1,0:T(8,128)}, f32[1,128]{1,0:T(1,128)}, /*index=5*/f32[1,8]{1,0:T(1,128)}) custom-call(f32[1,128,256]{2,1,0:T(8,128)} %feat_hbm.1, f32[3,1,256]{2,1,0:T(1,128)} %bitcast.5, s32[1,256]{1,0:T(1,128)} %spec_hbm.1, f32[1,256]{1,0:T(1,128)} %eg_hbm.1, ...), custom_call_target="tpu_custom_call" | custom-call | tf_op jit(solution)/shard_map/pallas_call | solution.py:607
  68.5 1.8 %shard_map.155 = (f32[1,256]{1,0:T(1,128)}, f32[1,128,256]{2,1,0:T(8,128)}, f32[8,128]{1,0:T(8,128)}, f32[384,128]{1,0:T(8,128)}, f32[1,128]{1,0:T(1,128)}, /*index=5*/f32[1,8]{1,0:T(1,128)}) custom-call(f32[1,256]{1,0:T(1,128)} %get-tuple-element.18.refs_0_, f32[1,128,256]{2,1,0:T(8,128)} %get-tuple-element.19.refs_1_, f32[8,128]{1,0:T(8,128)} %get-tuple-element.20.refs_2_, ...), custom_call_target="tpu_custom_call" | custom-call | tf_op jit(solution)/shard_map/pallas_call | solution.py:676
